TPU v7x, 128 devices: a whole 4x4x4 slice. The times are simulated.
128 devices in a mesh: basin: 32 (over z, x, core), tm: 4 (over y).
Axes of the slice: x: 4, y: 4, z: 4, core: 2. Of those that a mesh axis runs over, the one named last changes fastest.
Arguments:
- incidence: int32 [1024, 16, 128], P('basin'), may hold values 0 or 1
- row_gauge: int32 [16384], P('basin'), may hold values from 0 to 8191, as said below
- gauge_kernel: int32 [8192], P('basin'), may hold values from 0 to 31
- kernels: float32 [32, 128], replicated, may hold values from 0 to 0.0156
- observed: float32 [8192, 512], P('basin', 'tm'), may hold values from -8 to 8
- first_guess: float32 [131072, 512], P('basin', 'tm'), may hold values from -4 to 4
Outputs:
- inflows: float32 [131072, 512], P('basin', 'tm')
Inputs may be any that keep to these rules, and one draw needn't show every extreme that they name: `row_gauge`: the 512 slots of one index of basin name gauges of any one owner (gauges o * 256 to o * 256 + 255 belong to owner o) at most 32 times; in every draw one owner is named exactly 32 times by the slots of every index of basin.
All inputs are finite; a program needn't handle non-finite values. No bound on the sum of `incidence` on one device may be relied on, other than what follows from the above.
Results may differ from a plain program's by a relative error of at most 0.0001.
Values sent between devices are 32-bit elements; how exact they have to be, the bound alone decides.
A program may use at most 128 MiB of HBM per device.

v0:
```python
import jax
import jax.numpy as jnp
from jax import lax
from jax.sharding import PartitionSpec as P

ITERS = 3


HIGH = lax.Precision.HIGHEST


def from_behind(x, axis, by):
    devices = lax.axis_size(axis)
    pairs = [(i, i + by) for i in range(devices) if 0 <= i + by < devices]
    return lax.ppermute(x, axis, pairs)


def lag_table(kernels, lag):
    taps = kernels.shape[1]
    valid = (lag >= 0) & (lag < taps)
    picked = jnp.take(kernels, jnp.clip(lag, 0, taps - 1), axis=1)
    picked = jnp.where(valid[None, :, :], picked, 0.0)
    return jnp.transpose(picked, (1, 0, 2)).reshape(lag.shape[0], -1)


def class_mix(extended, table, selector):
    gauges = extended.shape[0]
    classes = selector.shape[1]
    spread = jnp.dot(extended, table, precision=HIGH).reshape(gauges, classes, -1)
    return jnp.einsum("gch,gc->gh", spread, selector, precision=HIGH)


def squared(values):
    return jnp.sum(values * values)


def gauge_total(value):
    return lax.psum(value, ("basin", "tm"))


def reach_total(value):
    return lax.psum(value, ("basin", "tm"))


def shards(incidence, row_gauge, gauge_kernel, kernels, observed, first_guess):
    weights = incidence.astype(jnp.float32)
    blocks, slots, width = weights.shape
    gauges_here, hours = observed.shape
    owners = lax.axis_size("basin")
    classes = kernels.shape[0]
    partials = blocks * slots
    outer = jnp.arange(2 * hours)[:, None]
    inner = jnp.arange(hours)[None, :]
    table_fwd = lag_table(kernels, inner + hours - outer)
    table_bwd = lag_table(kernels, outer - inner)
    selector = (gauge_kernel[:, None] == jnp.arange(classes)[None, :]).astype(jnp.float32)

    def to_gauges(partial_value):
        table = (
            jnp.zeros((gauges_here * owners, hours), jnp.float32).at[row_gauge].add(partial_value)
        )
        return lax.psum_scatter(table, "basin", scatter_dimension=0, tiled=True)

    def from_gauges(upstream):
        everything = lax.all_gather(upstream, "basin", axis=0, tiled=True)
        return everything[row_gauge]

    def forward(field):
        partial_value = jnp.einsum(
            "bjr,brt->bjt", weights, field.reshape(blocks, width, hours), precision=HIGH
        )
        sums = to_gauges(partial_value.reshape(partials, hours))
        earlier = from_behind(sums, "tm", 1)
        return class_mix(jnp.concatenate([earlier, sums], axis=1), table_fwd, selector)

    def backward(series):
        later = from_behind(series, "tm", -1)
        upstream = class_mix(jnp.concatenate([series, later], axis=1), table_bwd, selector)
        rows = from_gauges(upstream)
        spread = jnp.einsum(
            "bjr,bjt->brt", weights, rows.reshape(blocks, slots, hours), precision=HIGH
        )
        return spread.reshape(blocks * width, hours)

    start = observed - forward(first_guess)
    beta = jnp.sqrt(gauge_total(squared(start)))
    u = start / beta
    pulled = backward(u)
    alpha = jnp.sqrt(reach_total(squared(pulled)))
    v = pulled / alpha
    w = v
    correction = jnp.zeros(first_guess.shape, jnp.float32)
    phibar = beta
    rhobar = alpha
    for step in range(ITERS):
        final = step == ITERS - 1
        p = forward(v) - alpha * u
        beta = jnp.sqrt(gauge_total(squared(p)))
        if not final:
            pulled = backward(p / beta) - beta * v
            alpha_next = jnp.sqrt(reach_total(squared(pulled)))
            v_next = pulled / alpha_next
        u = p / beta
        rho = jnp.sqrt(rhobar * rhobar + beta * beta)
        cosine = rhobar / rho
        sine = beta / rho
        phi = cosine * phibar
        phibar = sine * phibar
        correction = correction + phi / rho * w
        if not final:
            theta = sine * alpha_next
            rhobar = -cosine * alpha_next
            w = v_next - theta / rho * w
            v = v_next
            alpha = alpha_next
    return first_guess + correction


def solution(mesh):
    in_specs = (
        P("basin", None, None),
        P("basin"),
        P("basin"),
        P(),
        P("basin", "tm"),
        P("basin", "tm"),
    )
    out_specs = P("basin", "tm")
    return jax.shard_map(shards, mesh=mesh, in_specs=in_specs, out_specs=out_specs, check_vma=False)
```

profile of v0, /device:TPU:1, one launch (start us, length us, event | category | flops | bytes accessed | tf_op | source)
XLA Modules:
  0.0 1270.0 jit_solution(18081621029645667303)
XLA Ops:
  6.5 0.7 compare_select_fusion.2
  7.2 3.5 fusion.88
  10.8 4.4 scatter_custom_fusion
  15.4 108.2 %gather_fusion.3 = f32[32768,32]{1,0:T(8,128)} fusion(f32[32,128]{0,1:T(8,128)S(1)} %copy.21, s32[32768]{0:T(1024)S(1)} %bitcast_clamp_fusion.1), kind=kCustom, calls=%fused_computation.clone | custom fusion | bytes 8519680 | tf_op jit(solution)/shard_map/jit(_take)/gather | solution.py:21
  123.7 14.0 %copy.22 = f32[256,128,32]{0,1,2:T(8,128)} copy(f32[256,128,32]{2,1,0:T(8,128)} %bitcast.119) | data formatting | bytes 8388608 | tf_op jit(solution)/shard_map/jit(_take)/gather | solution.py:21
  138.1 4.3 collective-permute-start
  142.6 2.0 collective-permute-done
  144.6 5.6 fusion.12
  150.2 4.4 fusion.26
  155.3 68.8 %psum.49 = f32[]{:T(128)} all-reduce(f32[]{:T(128)} %get-tuple-element.6), channel_id=1, replica_groups=mesh['basin'=32,'tm'=4] {'basin','tm'}, use_global_device_ids=true, to_apply=%region_3.5 | all-reduce | flops 1 | bytes 8 | tf_op jit(solution)/shard_map/psum | solution.py:38
  224.9 1.8 collective-permute-start.1
  226.7 108.2 %gather_fusion.4 = f32[32768,32]{1,0:T(8,128)} fusion(f32[32,128]{0,1:T(8,128)S(1)} %copy.21, s32[32768]{0:T(1024)S(1)} %bitcast_clamp_fusion), kind=kCustom, calls=%fused_computation.1.clone | custom fusion | bytes 8519680 | tf_op jit(solution)/shard_map/jit(_take)/gather | solution.py:21
  335.0 14.0 %copy.26 = f32[256,128,32]{0,1,2:T(8,128)} copy(f32[256,128,32]{2,1,0:T(8,128)} %bitcast.118) | data formatting | bytes 8388608 | tf_op jit(solution)/shard_map/jit(_take)/gather | solution.py:21
  349.3 5.6 fusion.4
  354.9 5.1 fusion.24
  360.1 45.8 %all-gather.4.cloned.1.call-done = f32[8192,128]{1,0:T(8,128)} async-done(((f32[256,128]{1,0:T(8,128)}), f32[8192,128]{1,0:T(8,128)}) %all-gather.4.cloned.1.call-update) | async-done | bytes 4194320 | tf_op jit(solution)/shard_map/all_gather | solution.py:65
  405.8 3.2 gather_fusion
  409.1 4.0 multiply_reduce_fusion.2
  413.1 64.3 %psum.50 = f32[]{:T(128)} all-reduce(f32[]{:T(128)} %get-tuple-element.10), channel_id=1, replica_groups=mesh['basin'=32,'tm'=4] {'basin','tm'}, use_global_device_ids=true, to_apply=%region_5.7 | all-reduce | flops 1 | bytes 8 | tf_op jit(solution)/shard_map/psum | solution.py:42
  478.1 2.0 fusion.84
  480.1 4.4 scatter_custom_fusion.1
  484.6 77.8 %reduce-scatter.7.cloned.1.call-done = f32[256,128]{1,0:T(8,128)} async-done(((f32[8192,128]{1,0:T(8,128)}), f32[256,128]{1,0:T(8,128)}) %reduce-scatter.7.cloned.1.call-update) | async-done | bytes 131088 | tf_op jit(solution)/shard_map/reduce_scatter | solution.py:62
  562.4 3.1 collective-permute-start.2
  565.5 2.2 collective-permute-done.2
  567.7 5.6 fusion.10
  573.3 4.4 fusion.22
  577.7 0.6 multiply_reduce_fusion.5
  578.4 67.6 %psum.51 = f32[]{:T(128)} all-reduce(f32[]{:T(128)} %multiply_reduce_fusion.5), channel_id=1, replica_groups=mesh['basin'=32,'tm'=4] {'basin','tm'}, use_global_device_ids=true, to_apply=%region_9.11 | all-reduce | flops 1 | bytes 8 | tf_op jit(solution)/shard_map/psum | solution.py:38
  646.7 1.7 collective-permute-start.3
  648.4 4.0 collective-permute-done.3
  652.5 5.6 fusion.2
  658.1 5.1 fusion.20
  663.2 44.6 %all-gather.6.cloned.1.call-done = f32[8192,128]{1,0:T(8,128)} async-done(((f32[256,128]{1,0:T(8,128)}), f32[8192,128]{1,0:T(8,128)}) %all-gather.6.cloned.1.call-update) | async-done | bytes 4194320 | tf_op jit(solution)/shard_map/all_gather | solution.py:65
  707.8 3.2 gather_fusion.1
  711.0 5.4 multiply_reduce_fusion.1
  716.4 64.3 %psum.52 = f32[]{:T(128)} all-reduce(f32[]{:T(128)} %get-tuple-element.12), channel_id=1, replica_groups=mesh['basin'=32,'tm'=4] {'basin','tm'}, use_global_device_ids=true, to_apply=%region_11.13 | all-reduce | flops 1 | bytes 8 | tf_op jit(solution)/shard_map/psum | solution.py:42
  781.4 3.6 fusion.81
  784.9 4.4 scatter_custom_fusion.2
  789.4 77.7 %reduce-scatter.9.cloned.1.call-done = f32[256,128]{1,0:T(8,128)} async-done(((f32[8192,128]{1,0:T(8,128)}), f32[256,128]{1,0:T(8,128)}) %reduce-scatter.9.cloned.1.call-update) | async-done | bytes 131088 | tf_op jit(solution)/shard_map/reduce_scatter | solution.py:62
  867.1 3.1 collective-permute-start.4
  870.3 2.2 collective-permute-done.4
  872.5 5.6 fusion.8
  878.1 4.4 fusion.18
  882.5 0.7 multiply_reduce_fusion.4
  883.3 67.6 %psum.53 = f32[]{:T(128)} all-reduce(f32[]{:T(128)} %multiply_reduce_fusion.4), channel_id=1, replica_groups=mesh['basin'=32,'tm'=4] {'basin','tm'}, use_global_device_ids=true, to_apply=%region_15.17 | all-reduce | flops 1 | bytes 8 | tf_op jit(solution)/shard_map/psum | solution.py:38
  951.7 1.5 collective-permute-start.5
  953.2 4.2 collective-permute-done.5
  957.4 5.6 fusion
  963.0 5.1 fusion.16
  968.1 44.6 %all-gather.8.cloned.1.call-done = f32[8192,128]{1,0:T(8,128)} async-done(((f32[256,128]{1,0:T(8,128)}), f32[8192,128]{1,0:T(8,128)}) %all-gather.8.cloned.1.call-update) | async-done | bytes 4194320 | tf_op jit(solution)/shard_map/all_gather | solution.py:65
  1012.7 3.2 gather_fusion.2
  1015.9 6.6 multiply_reduce_fusion
  1022.5 64.6 %psum.54 = f32[]{:T(128)} all-reduce(f32[]{:T(128)} %get-tuple-element.14), channel_id=1, replica_groups=mesh['basin'=32,'tm'=4] {'basin','tm'}, use_global_device_ids=true, to_apply=%region_17.19 | all-reduce | flops 1 | bytes 8 | tf_op jit(solution)/shard_map/psum | solution.py:42
  1087.7 3.6 fusion.64
  1091.2 4.4 scatter_custom_fusion.3
  1095.7 77.8 %reduce-scatter.11.cloned.1.call-done = f32[256,128]{1,0:T(8,128)} async-done(((f32[8192,128]{1,0:T(8,128)}), f32[256,128]{1,0:T(8,128)}) %reduce-scatter.11.cloned.1.call-update) | async-done | bytes 131088 | tf_op jit(solution)/shard_map/reduce_scatter | solution.py:62
  1173.5 3.3 collective-permute-start.6
  1177.2 1.7 collective-permute-done.6
  1178.8 5.6 fusion.6
  1184.5 4.4 fusion.14
  1188.9 0.7 multiply_reduce_fusion.3
  1189.6 67.7 %psum.55 = f32[]{:T(128)} all-reduce(f32[]{:T(128)} %multiply_reduce_fusion.3), channel_id=1, replica_groups=mesh['basin'=32,'tm'=4] {'basin','tm'}, use_global_device_ids=true, to_apply=%region_21.23 | all-reduce | flops 1 | bytes 8 | tf_op jit(solution)/shard_map/psum | solution.py:38
  1258.2 3.2 multiply_add_fusion
  1261.4 1.5 bitcast_add_fusion
  (43 shorter events, 2.1 us)
Async XLA Ops:
  6.5 131.6 %reduce-scatter.5.cloned.1.call-start = ((), (), s32[]{:S(2)}) async-start(), calls=%async_computation.4 | async-start | bytes 4325376 | tf_op jit(solution)/shard_map/reduce_scatter | solution.py:62
  10.7 4.5 copy-start.3
  15.2 390.6 %all-gather.4.cloned.1.call-start = ((), (), s32[]{:S(2)}) async-start(), calls=%async_computation.5 | async-start | bytes 4325376 | tf_op jit(solution)/shard_map/all_gather | solution.py:65
  123.7 18.8 %copy-start.4 = (s32[256]{0:T(256)S(1)}, s32[256]{0:T(256)}, u32[]{:S(2)}) copy-start(s32[256]{0:T(256)} %param.10) | copy-start | bytes 3076
  138.1 6.5 collective-permute-start
  150.2 4.4 copy-start.2
  224.9 124.4 %collective-permute-start.1 = (f32[256,128]{1,0:T(8,128)S(1)}, f32[256,128]{1,0:T(8,128)S(1)}, u32[]{:S(2)}, u32[]{:S(2)}) collective-permute-start(f32[256,128]{1,0:T(8,128)S(1)} %broadcast_divide_fusion.6), channel_id=1, source_target_pairs={{1,0},{2,1},{3,2},{5,4},{6,5},{7,6},{9,8},{10,9},{11,10},{13,12},{... | collective-permute-start | bytes 393224 | tf_op jit(solution)/shard_map/ppermute | solution.py:15
  354.9 54.2 %copy-start.1 = (s32[32,16,128]{2,1,0:T(8,128)S(1)}, s32[32,16,128]{2,1,0:T(8,128)}, u32[]{:S(2)}) copy-start(s32[32,16,128]{2,1,0:T(8,128)} %param.8) | copy-start | bytes 786436
  360.0 202.3 %reduce-scatter.7.cloned.1.call-start = ((), (), s32[]{:S(2)}) async-start(), calls=%async_computation.6 | async-start | bytes 4325376 | tf_op jit(solution)/shard_map/reduce_scatter | solution.py:62
  484.5 223.2 %all-gather.6.cloned.1.call-start = ((), (), s32[]{:S(2)}) async-start(), calls=%async_computation.7 | async-start | bytes 4325376 | tf_op jit(solution)/shard_map/all_gather | solution.py:65
  562.4 5.4 collective-permute-start.2
  646.7 5.7 collective-permute-start.3
  663.2 204.0 %reduce-scatter.9.cloned.1.call-start = ((), (), s32[]{:S(2)}) async-start(), calls=%async_computation.8 | async-start | bytes 4325376 | tf_op jit(solution)/shard_map/reduce_scatter | solution.py:62
  789.4 223.3 %all-gather.8.cloned.1.call-start = ((), (), s32[]{:S(2)}) async-start(), calls=%async_computation.9 | async-start | bytes 4325376 | tf_op jit(solution)/shard_map/all_gather | solution.py:65
  867.1 5.4 collective-permute-start.4
  951.7 5.7 collective-permute-start.5
  968.1 205.4 %reduce-scatter.11.cloned.1.call-start = ((), (), s32[]{:S(2)}) async-start(), calls=%async_computation.10 | async-start | bytes 4325376 | tf_op jit(solution)/shard_map/reduce_scatter | solution.py:62
  1173.5 5.3 collective-permute-start.6
  1258.2 3.2 copy-start
Sparse Core Ops, SparseCore 0:
  15.3 83.6 reduce-scatter.4
  360.1 45.6 all-gather.3
  484.7 77.6 reduce-scatter.6
  663.3 44.4 all-gather.5
  789.5 77.6 reduce-scatter.8
  968.2 44.4 all-gather.7
  1095.8 77.6 reduce-scatter.10
where the time goes:
time: 1280 us; the launch traced here: 1270 us
  blocking collectives  465 us (36%)
  waiting for transfers between devices  385 us (30%)
  local copies, waits for them, and re-layouts  255 us (20%)
  matrix products  101 us (8%)
  other arithmetic  26.2 us (2%)
  between operations  19.3 us (2%)
  starting transfers between devices  19.1 us (1%)
    psum x4, blocking collectives, gauge_total(): return lax.psum(value, ('basin', 'tm'))  272 us
    gather x4, local copies, waits for them, and re-layouts, lag_table(): picked = jnp.take(kernels, jnp.clip(lag, 0, taps - 1), axis=1)  244 us
    reduce_scatter x4, waiting for transfers between devices, to_gauges(): return lax.psum_scatter(table, 'basin', scatter_dimension=0, tiled=True)  233 us
    psum x3, blocking collectives, reach_total(): return lax.psum(value, ('basin', 'tm'))  193 us
    all_gather x3, waiting for transfers between devices, from_gauges(): everything = lax.all_gather(upstream, 'basin', axis=0, tiled=True)  135 us
    dot_general x7, matrix products, class_mix(): jnp.dot(extended, table, precision=HIGH).reshape(gauges, classes, -1)  39.2 us
    dot_general x7, matrix products, class_mix(): return jnp.einsum('gch,gc->gh', spread, selector, precision=HIGH)  32.9 us
  transfers between devices with their start and end apart: 14, of which 12 were waited for; matrix products, arithmetic and copies ran while one was open for 19% of the time, Pallas kernels for 0%

commit v1 on v0

--- a/solution.py
+++ b/solution.py
@@ -1,12 +1,18 @@
+import functools
+
 import jax
 import jax.numpy as jnp
 from jax import lax
+from jax.experimental import pallas as pl
+from jax.experimental.pallas import tpu as pltpu
 from jax.sharding import PartitionSpec as P
 
 ITERS = 3
-
+CAP = 32
+LANES = 128
 
 HIGH = lax.Precision.HIGHEST
+MESH = pl.DeviceIdType.MESH
 
 
 def from_behind(x, axis, by):
@@ -16,30 +22,80 @@
 
 
 def lag_table(kernels, lag):
-    taps = kernels.shape[1]
-    valid = (lag >= 0) & (lag < taps)
-    picked = jnp.take(kernels, jnp.clip(lag, 0, taps - 1), axis=1)
-    picked = jnp.where(valid[None, :, :], picked, 0.0)
-    return jnp.transpose(picked, (1, 0, 2)).reshape(lag.shape[0], -1)
+    classes, taps = kernels.shape
+    rows, hours = lag.shape
+    onehot = (lag[None, :, :] == jnp.arange(taps)[:, None, None]).astype(jnp.float32)
+    picked = jnp.dot(kernels, onehot.reshape(taps, rows * hours), precision=HIGH)
+    picked = picked.reshape(classes, rows, hours)
+    return jnp.transpose(picked, (1, 0, 2)).reshape(rows, classes * hours)
 
 
 def class_mix(extended, table, selector):
     gauges = extended.shape[0]
     classes = selector.shape[1]
     spread = jnp.dot(extended, table, precision=HIGH).reshape(gauges, classes, -1)
-    return jnp.einsum("gch,gc->gh", spread, selector, precision=HIGH)
+    return jnp.sum(spread * selector[:, :, None], axis=1)
 
 
 def squared(values):
     return jnp.sum(values * values)
 
 
-def gauge_total(value):
-    return lax.psum(value, ("basin", "tm"))
+def _allreduce_body(x_ref, o_ref, buf, own_sem, send_sem, recv_sem, *, nb, nt, rounds):
+    me = lax.axis_index("basin") * nt + lax.axis_index("tm")
+
+    def peer(r):
+        step = 1 << r
+        bit = (me // step) % 2
+        other = me + step - 2 * step * bit
+        return (other // nt, other % nt)
+
+    barrier = pltpu.get_barrier_semaphore()
+    for r in range(rounds):
+        pl.semaphore_signal(barrier, inc=1, device_id=peer(r), device_id_type=MESH)
+    pl.semaphore_wait(barrier, rounds)
+
+    own = pltpu.make_async_copy(x_ref, buf.at[pl.ds(me, 1)], own_sem)
+    own.start()
+    own.wait()
+    for r in range(rounds):
+        step = 1 << r
+        base = (me // step) * step
+        copy = pltpu.make_async_remote_copy(
+            src_ref=buf.at[pl.ds(base, step)],
+            dst_ref=buf.at[pl.ds(base, step)],
+            send_sem=send_sem.at[r],
+            recv_sem=recv_sem.at[r],
+            device_id=peer(r),
+            device_id_type=MESH,
+        )
+        copy.start()
+        copy.wait()
+    o_ref[...] = jnp.sum(buf[...], axis=0, keepdims=True)
 
 
-def reach_total(value):
-    return lax.psum(value, ("basin", "tm"))
+def global_total(value):
+    nb = lax.axis_size("basin")
+    nt = lax.axis_size("tm")
+    n = nb * nt
+    rounds = n.bit_length() - 1
+    if n != (1 << rounds) or n < 2:
+        return lax.psum(value, ("basin", "tm"))
+    x = jnp.broadcast_to(value.astype(jnp.float32), (1, LANES))
+    out = pl.pallas_call(
+        functools.partial(_allreduce_body, nb=nb, nt=nt, rounds=rounds),
+        out_shape=jax.ShapeDtypeStruct((1, LANES), jnp.float32),
+        in_specs=[pl.BlockSpec(memory_space=pltpu.VMEM)],
+        out_specs=pl.BlockSpec(memory_space=pltpu.VMEM),
+        scratch_shapes=[
+            pltpu.VMEM((n, LANES), jnp.float32),
+            pltpu.SemaphoreType.DMA(()),
+            pltpu.SemaphoreType.DMA((rounds,)),
+            pltpu.SemaphoreType.DMA((rounds,)),
+        ],
+        compiler_params=pltpu.CompilerParams(collective_id=0, has_side_effects=True),
+    )(x)
+    return out[0, 0]
 
 
 def shards(incidence, row_gauge, gauge_kernel, kernels, observed, first_guess):
@@ -55,15 +111,26 @@
     table_bwd = lag_table(kernels, outer - inner)
     selector = (gauge_kernel[:, None] == jnp.arange(classes)[None, :]).astype(jnp.float32)
 
+    owner = row_gauge // gauges_here
+    local = row_gauge % gauges_here
+    hit = owner[:, None] == jnp.arange(owners)[None, :]
+    rank = jnp.cumsum(hit.astype(jnp.int32), axis=0) - 1
+    dest = owner * CAP + jnp.sum(jnp.where(hit, rank, 0), axis=1)
+    entries = owners * CAP
+    place = (jnp.arange(entries)[:, None] == dest[None, :]).astype(jnp.float32)
+    sent_ids = jnp.full((entries,), -1, jnp.int32).at[dest].set(local)
+    got_ids = lax.all_to_all(sent_ids, "basin", 0, 0, tiled=True)
+    gather = (jnp.arange(gauges_here)[:, None] == got_ids[None, :]).astype(jnp.float32)
+
     def to_gauges(partial_value):
-        table = (
-            jnp.zeros((gauges_here * owners, hours), jnp.float32).at[row_gauge].add(partial_value)
-        )
-        return lax.psum_scatter(table, "basin", scatter_dimension=0, tiled=True)
+        outgoing = jnp.dot(place, partial_value, precision=HIGH)
+        incoming = lax.all_to_all(outgoing, "basin", 0, 0, tiled=True)
+        return jnp.dot(gather, incoming, precision=HIGH)
 
     def from_gauges(upstream):
-        everything = lax.all_gather(upstream, "basin", axis=0, tiled=True)
-        return everything[row_gauge]
+        outgoing = jnp.dot(gather.T, upstream, precision=HIGH)
+        incoming = lax.all_to_all(outgoing, "basin", 0, 0, tiled=True)
+        return jnp.dot(place.T, incoming, precision=HIGH)
 
     def forward(field):
         partial_value = jnp.einsum(
@@ -83,10 +150,10 @@
         return spread.reshape(blocks * width, hours)
 
     start = observed - forward(first_guess)
-    beta = jnp.sqrt(gauge_total(squared(start)))
+    beta = jnp.sqrt(global_total(squared(start)))
     u = start / beta
     pulled = backward(u)
-    alpha = jnp.sqrt(reach_total(squared(pulled)))
+    alpha = jnp.sqrt(global_total(squared(pulled)))
     v = pulled / alpha
     w = v
     correction = jnp.zeros(first_guess.shape, jnp.float32)
@@ -95,10 +162,10 @@
     for step in range(ITERS):
         final = step == ITERS - 1
         p = forward(v) - alpha * u
-        beta = jnp.sqrt(gauge_total(squared(p)))
+        beta = jnp.sqrt(global_total(squared(p)))
         if not final:
             pulled = backward(p / beta) - beta * v
-            alpha_next = jnp.sqrt(reach_total(squared(pulled)))
+            alpha_next = jnp.sqrt(global_total(squared(pulled)))
             v_next = pulled / alpha_next
         u = p / beta
         rho = jnp.sqrt(rhobar * rhobar + beta * beta)

time: 1280 us -> 475 us (0.37)
  blocking collectives: 465 us -> 102 us
  waiting for transfers between devices: 385 us -> 30.3 us
  local copies, waits for them, and re-layouts: 255 us -> 28.6 us
  Pallas kernels: 0 us -> 147 us
  starting transfers between devices: 19.1 us -> 38.3 us
  other arithmetic: 26.2 us -> 10.5 us
  between operations: 19.3 us -> 5.87 us
    psum x7 -> x0, blocking collectives: 465 us -> none  [the longest x4 272 us: gauge_total(): return lax.psum(value, ('basin', 'tm'))]
    gather x7 -> x0, local copies, waits for them, and re-layouts: 254 us -> none  [the longest x4 244 us: lag_table(): picked = jnp.take(kernels, jnp.clip(lag, 0, taps - 1), axis=1)]
    reduce_scatter x4 -> x0, waiting for transfers between devices: 233 us -> none  [to_gauges(): return lax.psum_scatter(table, 'basin', scatter_dimension=0, tiled=True)]
    pallas_call x0 -> x7, Pallas kernels: none -> 147 us  [global_total(): pl.pallas_call(functools.partial(_allreduce_body, nb=nb, nt=nt, rounds=ro...]
    all_gather x3 -> x0, waiting for transfers between devices: 135 us -> none  [from_gauges(): everything = lax.all_gather(upstream, 'basin', axis=0, tiled=True)]
    all_to_all x0 -> x5, blocking collectives: none -> 102 us  [the longest x3 61.5 us: to_gauges(): incoming = lax.all_to_all(outgoing, 'basin', 0, 0, tiled=True)]
    all_to_all x0 -> x3, starting transfers between devices: none -> 23.2 us  [the longest x1 9.43 us: shards(): got_ids = lax.all_to_all(sent_ids, 'basin', 0, 0, tiled=True)]
    scatter-add x4 -> x0, other arithmetic: 17.6 us -> none  [to_gauges(): jnp.zeros((gauges_here * owners, hours), jnp.float32).at[row_gauge]]
  transfers between devices with their start and end apart: 14 -> 10, of which waited for: 12 -> 8; matrix products, arithmetic and copies ran while one was open for 19% -> 8% of each run, Pallas kernels for 0% -> 0%
where the time goes in v1:
time: 475 us; the launch traced here: 467 us
  Pallas kernels  147 us (31%)
  matrix products  104 us (22%)
  blocking collectives  102 us (21%)
  starting transfers between devices  38.3 us (8%)
  waiting for transfers between devices  30.3 us (6%)
  local copies, waits for them, and re-layouts  28.6 us (6%)
  other arithmetic  10.5 us (2%)
  between operations  5.87 us (1%)
    pallas_call x7, Pallas kernels, global_total(): pl.pallas_call(functools.partial(_allreduce_body, nb=nb, nt=nt, rounds=ro...  147 us
    all_to_all x3, blocking collectives, to_gauges(): incoming = lax.all_to_all(outgoing, 'basin', 0, 0, tiled=True)  61.5 us
    dot_general x7, matrix products, class_mix(): jnp.dot(extended, table, precision=HIGH).reshape(gauges, classes, -1)  51.7 us
    all_to_all x2, blocking collectives, from_gauges(): incoming = lax.all_to_all(outgoing, 'basin', 0, 0, tiled=True)  40.7 us
    ppermute x7, waiting for transfers between devices, from_behind(): return lax.ppermute(x, axis, pairs)  17.7 us
    ppermute x7, starting transfers between devices, from_behind(): return lax.ppermute(x, axis, pairs)  15.1 us
    dot_general x3, matrix products, backward(): jnp.einsum('bjr,bjt->brt', weights, rows.reshape(blocks, slots, hours), p...  14.8 us
    dot_general x4, matrix products, forward(): jnp.einsum('bjr,brt->bjt', weights, field.reshape(blocks, width, hours),...  12.8 us
  transfers between devices with their start and end apart: 10, of which 8 were waited for; matrix products, arithmetic and copies ran while one was open for 8% of the time, Pallas kernels for 0%

profile of v1, /device:TPU:1, one launch (start us, length us, event | category | flops | bytes accessed | tf_op | source)
XLA Modules:
  0.0 467.2 jit_solution(15729893750899146629)
XLA Ops:
  0.7 1.2 reduce-window.6
  2.3 2.4 scatter_custom_fusion
  5.4 9.4 %all-to-all-start = ((s32[32,32,1]{1,2,0:T(1,128)}), s32[32,32,1]{1,2,0:T(1,128)S(1)}, u32[]{:S(2)}, u32[]{:S(2)}) async-start(s32[32,32,1]{1,2,0:T(1,128)} %all_to_all.48), calls=%async_computation | async-start | bytes 32768 | tf_op jit(solution)/shard_map/all_to_all | solution.py:122
  14.9 3.5 fusion.88
  18.4 1.8 fusion.24
  20.3 1.5 all-to-all-done
  21.8 6.3 %all-to-all-start.1 = ((f32[32,32,128]{2,1,0:T(8,128)}), f32[32,32,128]{2,1,0:T(8,128)S(1)}, u32[]{:S(2)}, u32[]{:S(2)}) async-start(f32[32,32,128]{2,1,0:T(8,128)} %fusion.24), calls=%async_computation.1 | async-start | bytes 1048576 | tf_op jit(solution)/shard_map/all_to_all | solution.py:127
  28.1 5.8 %fusion.27 = f32[4,8,256,128]{3,1,2,0:T(8,128)S(1)} fusion(f32[32,128]{1,0:T(8,128)S(1)} %copy-done, s32[32768]{0:T(1024)S(1)} %subtract_bitcast_fusion.1), kind=kOutput, calls=%fused_computation.37 | convolution fusion | flops 1614807040 | bytes 4341760 | tf_op jit(solution)/shard_map/dot_general | solution.py:28
  33.8 2.7 copy.46
  36.6 5.6 %copy.25 = f32[32,256,128]{1,2,0:T(8,128)} copy(f32[32,256,128]{2,1,0:T(8,128)} %bitcast.173) | data formatting | bytes 8388608 | tf_op jit(solution)/shard_map/reshape | solution.py:29
  44.1 3.2 collective-permute-start
  47.4 2.7 collective-permute-done
  50.1 9.4 %multiply_reduce_fusion.6 = f32[256,128]{1,0:T(8,128)S(1)} fusion(f32[32,256,128]{1,2,0:T(8,128)} %copy.25, f32[256,32]{0,1:T(8,128)S(1)} %fusion.96, f32[256,128]{0,1:T(8,128)S(1)} %fusion.53, f32[256,128]{0,1:T(8,128)S(1)} %collective-permute-done), kind=kOutput, calls=%fused_computation.27 | convolution fusion | flops 3223355392 | bytes 4620288 | tf_op jit(solution)/shard_map/dot_general | solution.py:36
  60.1 1.2 broadcast_in_dim.25.x_ref
  61.3 24.8 %shard_map.64 = f32[1,128]{1,0:T(1,128)} custom-call(f32[1,128]{1,0:T(1,128)} %broadcast_in_dim.25.x_ref), custom_call_target="tpu_custom_call" | custom-call | tf_op jit(solution)/shard_map/pallas_call | solution.py:85
  86.8 1.8 collective-permute-start.1
  88.6 5.8 %fusion.26 = f32[4,8,256,128]{3,1,2,0:T(8,128)S(1)} fusion(f32[32,128]{1,0:T(8,128)S(1)} %copy-done, s32[32768]{0:T(1024)S(1)} %subtract_bitcast_fusion), kind=kOutput, calls=%fused_computation.36 | convolution fusion | flops 1614807040 | bytes 4341760 | tf_op jit(solution)/shard_map/dot_general | solution.py:28
  94.4 2.7 copy.47
  97.1 5.6 %copy.27 = f32[32,256,128]{1,2,0:T(8,128)} copy(f32[32,256,128]{2,1,0:T(8,128)} %bitcast.174) | data formatting | bytes 8388608 | tf_op jit(solution)/shard_map/reshape | solution.py:29
  102.7 5.7 %multiply_reduce_fusion.5 = f32[256,128]{1,0:T(8,128)S(1)} fusion(f32[32,256,128]{1,2,0:T(8,128)} %copy.27, f32[256,32]{0,1:T(8,128)S(1)} %fusion.96, f32[256,128]{1,0:T(8,128)S(1)} %collective-permute-done.1, f32[256,128]{1,0:T(8,128)S(1)} %broadcast_divide_fusion.6), kind=kOutput, calls=%fused_computation.26 | convolution fusion | flops 3223355392 | bytes 4620288 | tf_op jit(solution)/shard_map/dot_general | solution.py:36
  108.4 1.4 fusion.56
  109.9 7.5 %all-to-all-start.2 = ((f32[32,32,128]{2,1,0:T(8,128)}), f32[32,32,128]{2,1,0:T(8,128)S(1)}, u32[]{:S(2)}, u32[]{:S(2)}) async-start(f32[32,32,128]{2,1,0:T(8,128)} %fusion.56), calls=%async_computation.2 | async-start | bytes 1048576 | tf_op jit(solution)/shard_map/all_to_all | solution.py:132
  117.8 11.1 %all-to-all-done.2 = f32[32,32,128]{2,1,0:T(8,128)S(1)} async-done(((f32[32,32,128]{2,1,0:T(8,128)}), f32[32,32,128]{2,1,0:T(8,128)S(1)}, u32[]{:S(2)}, u32[]{:S(2)}) %all-to-all-start.2) | async-done | bytes 524320 | tf_op jit(solution)/shard_map/all_to_all | solution.py:132
  129.8 4.0 multiply_reduce_fusion.9
  133.9 1.1 broadcast_in_dim.26.x_ref
  135.0 20.3 %shard_map.65 = f32[1,128]{1,0:T(1,128)} custom-call(f32[1,128]{1,0:T(1,128)} %broadcast_in_dim.26.x_ref), custom_call_target="tpu_custom_call" | custom-call | tf_op jit(solution)/shard_map/pallas_call | solution.py:85
  156.0 2.0 fusion.84
  158.0 1.0 fusion.22
  159.0 20.5 %all_to_all.72 = f32[32,32,128]{2,1,0:T(8,128)S(1)} all-to-all(f32[32,32,128]{2,1,0:T(8,128)S(1)} %fusion.22), channel_id=1, replica_groups=mesh['basin'=32,'tm'=4] {'basin'}, dimensions={0} | all-to-all | bytes 1048576 | tf_op jit(solution)/shard_map/all_to_all | solution.py:127
  180.2 1.5 collective-permute-start.2
  181.7 2.5 collective-permute-done.2
  184.2 7.9 %multiply_reduce_fusion.4 = f32[256,128]{1,0:T(8,128)S(1)} fusion(f32[32,256,128]{1,2,0:T(8,128)S(1)} %copy-done.1, f32[256,32]{0,1:T(8,128)S(1)} %fusion.96, f32[256,128]{0,1:T(8,128)S(1)} %fusion.52, f32[256,128]{0,1:T(8,128)S(1)} %collective-permute-done.2), kind=kOutput, calls=%fused_computation.25 | convolution fusion | flops 3223355392 | bytes 4620288 | tf_op jit(solution)/shard_map/dot_general | solution.py:36
  192.8 1.2 broadcast_in_dim.27.x_ref
  194.0 22.2 %shard_map.66 = f32[1,128]{1,0:T(1,128)} custom-call(f32[1,128]{1,0:T(1,128)} %broadcast_in_dim.27.x_ref), custom_call_target="tpu_custom_call" | custom-call | tf_op jit(solution)/shard_map/pallas_call | solution.py:85
  216.9 1.3 collective-permute-start.3
  218.2 4.4 collective-permute-done.3
  222.6 5.7 %multiply_reduce_fusion.3 = f32[256,128]{1,0:T(8,128)S(1)} fusion(f32[32,256,128]{1,2,0:T(8,128)} %copy.27, f32[256,32]{0,1:T(8,128)S(1)} %fusion.96, f32[256,128]{1,0:T(8,128)S(1)} %collective-permute-done.3, f32[256,128]{1,0:T(8,128)S(1)} %broadcast_divide_fusion.5), kind=kOutput, calls=%fused_computation.24 | convolution fusion | flops 3223355392 | bytes 4620288 | tf_op jit(solution)/shard_map/dot_general | solution.py:36
  228.9 20.4 %all_to_all.73 = f32[32,32,128]{2,1,0:T(8,128)S(1)} all-to-all(f32[32,32,128]{2,1,0:T(8,128)S(1)} %fusion.55), channel_id=1, replica_groups=mesh['basin'=32,'tm'=4] {'basin'}, dimensions={0} | all-to-all | bytes 1048576 | tf_op jit(solution)/shard_map/all_to_all | solution.py:132
  250.3 5.4 %multiply_reduce_fusion.8 = (f32[]{:T(128)}, f32[32,128,128]{1,2,0:T(8,128)}) fusion(f32[32,128,128]{1,2,0:T(8,128)S(1)} %get-tuple-element.12, f32[]{:T(128)} %bitcast.26, f32[]{:T(128)} %bitcast.35, f32[32,16,128]{2,1,0:T(8,128)S(1)} %fusion.108, s32[32,16,128]{2,1,0:T(8,128)S(1)} %copy-done.5), kind=kOutput, calls=%fused_computation.42 | convolution fusion | flops 103350272 | bytes 4718604 | tf_op jit(solution)/shard_map/bjr,bjt->brt/dot_general | solution.py:147
  255.7 1.1 broadcast_in_dim.28.x_ref
  256.8 17.5 %shard_map.67 = f32[1,128]{1,0:T(1,128)} custom-call(f32[1,128]{1,0:T(1,128)} %broadcast_in_dim.28.x_ref), custom_call_target="tpu_custom_call" | custom-call | tf_op jit(solution)/shard_map/pallas_call | solution.py:85
  275.0 3.7 fusion.81
  279.8 20.5 %all_to_all.74 = f32[32,32,128]{2,1,0:T(8,128)S(1)} all-to-all(f32[32,32,128]{2,1,0:T(8,128)S(1)} %fusion.20), channel_id=1, replica_groups=mesh['basin'=32,'tm'=4] {'basin'}, dimensions={0} | all-to-all | bytes 1048576 | tf_op jit(solution)/shard_map/all_to_all | solution.py:127
  301.0 3.1 collective-permute-start.4
  304.1 1.9 collective-permute-done.4
  306.0 7.9 %multiply_reduce_fusion.2 = f32[256,128]{1,0:T(8,128)S(1)} fusion(f32[32,256,128]{1,2,0:T(8,128)S(1)} %copy-done.2, f32[256,32]{0,1:T(8,128)S(1)} %fusion.96, f32[256,128]{0,1:T(8,128)S(1)} %fusion.51, f32[256,128]{0,1:T(8,128)S(1)} %collective-permute-done.4), kind=kOutput, calls=%fused_computation.23 | convolution fusion | flops 3223355392 | bytes 4620288 | tf_op jit(solution)/shard_map/dot_general | solution.py:36
  314.6 1.1 broadcast_in_dim.29.x_ref
  315.6 22.4 %shard_map.68 = f32[1,128]{1,0:T(1,128)} custom-call(f32[1,128]{1,0:T(1,128)} %broadcast_in_dim.29.x_ref), custom_call_target="tpu_custom_call" | custom-call | tf_op jit(solution)/shard_map/pallas_call | solution.py:85
  338.7 1.3 collective-permute-start.5
  340.0 4.4 collective-permute-done.5
  344.4 5.7 %multiply_reduce_fusion.1 = f32[256,128]{1,0:T(8,128)S(1)} fusion(f32[32,256,128]{1,2,0:T(8,128)} %copy.27, f32[256,32]{0,1:T(8,128)S(1)} %fusion.96, f32[256,128]{1,0:T(8,128)S(1)} %collective-permute-done.5, f32[256,128]{1,0:T(8,128)S(1)} %broadcast_divide_fusion.4), kind=kOutput, calls=%fused_computation.22 | convolution fusion | flops 3223355392 | bytes 4620288 | tf_op jit(solution)/shard_map/dot_general | solution.py:36
  350.7 20.3 %all_to_all.75 = f32[32,32,128]{2,1,0:T(8,128)S(1)} all-to-all(f32[32,32,128]{2,1,0:T(8,128)S(1)} %fusion.54), channel_id=1, replica_groups=mesh['basin'=32,'tm'=4] {'basin'}, dimensions={0} | all-to-all | bytes 1048576 | tf_op jit(solution)/shard_map/all_to_all | solution.py:132
  372.1 5.4 %multiply_reduce_fusion.7 = (f32[]{:T(128)}, f32[32,128,128]{1,2,0:T(8,128)}) fusion(f32[32,128,128]{1,2,0:T(8,128)S(1)} %copy-done.4, f32[]{:T(128)} %bitcast.43, f32[]{:T(128)} %bitcast.49, f32[32,16,128]{2,1,0:T(8,128)S(1)} %fusion.109, s32[32,16,128]{2,1,0:T(8,128)S(1)} %copy-done.5), kind=kOutput, calls=%fused_computation.40 | convolution fusion | flops 103350272 | bytes 4718604 | tf_op jit(solution)/shard_map/bjr,bjt->brt/dot_general | solution.py:147
  377.5 1.1 broadcast_in_dim.30.x_ref
  378.6 17.6 %shard_map.69 = f32[1,128]{1,0:T(1,128)} custom-call(f32[1,128]{1,0:T(1,128)} %broadcast_in_dim.30.x_ref), custom_call_target="tpu_custom_call" | custom-call | tf_op jit(solution)/shard_map/pallas_call | solution.py:85
  396.8 3.6 fusion.57
  401.4 20.5 %all_to_all.76 = f32[32,32,128]{2,1,0:T(8,128)S(1)} all-to-all(f32[32,32,128]{2,1,0:T(8,128)S(1)} %fusion.18), channel_id=1, replica_groups=mesh['basin'=32,'tm'=4] {'basin'}, dimensions={0} | all-to-all | bytes 1048576 | tf_op jit(solution)/shard_map/all_to_all | solution.py:127
  422.6 2.8 collective-permute-start.6
  425.9 1.7 collective-permute-done.6
  427.7 9.4 %multiply_reduce_fusion = f32[256,128]{1,0:T(8,128)S(1)} fusion(f32[32,256,128]{1,2,0:T(8,128)} %copy.25, f32[256,32]{0,1:T(8,128)S(1)} %fusion.96, f32[256,128]{0,1:T(8,128)S(1)} %fusion.50, f32[256,128]{0,1:T(8,128)S(1)} %collective-permute-done.6), kind=kOutput, calls=%fused_computation.21 | convolution fusion | flops 3223355392 | bytes 4620288 | tf_op jit(solution)/shard_map/dot_general | solution.py:36
  437.7 1.2 broadcast_in_dim.31.x_ref
  438.9 22.6 %shard_map.70 = f32[1,128]{1,0:T(1,128)} custom-call(f32[1,128]{1,0:T(1,128)} %broadcast_in_dim.31.x_ref), custom_call_target="tpu_custom_call" | custom-call | tf_op jit(solution)/shard_map/pallas_call | solution.py:85
  462.3 3.2 multiply_add_fusion
  465.5 1.5 bitcast_add_fusion
  (53 shorter events, 15.2 us)
Async XLA Ops:
  0.0 28.1 %copy-start = (f32[32,128]{1,0:T(8,128)S(1)}, f32[32,128]{1,0:T(8,128)}, u32[]{:S(2)}) copy-start(f32[32,128]{1,0:T(8,128)} %param.9) | copy-start | bytes 49156
  5.4 16.4 %all-to-all-start = ((s32[32,32,1]{1,2,0:T(1,128)}), s32[32,32,1]{1,2,0:T(1,128)S(1)}, u32[]{:S(2)}, u32[]{:S(2)}) async-start(s32[32,32,1]{1,2,0:T(1,128)} %all_to_all.48), calls=%async_computation | async-start | bytes 32768 | tf_op jit(solution)/shard_map/all_to_all | solution.py:122
  21.8 21.7 %all-to-all-start.1 = ((f32[32,32,128]{2,1,0:T(8,128)}), f32[32,32,128]{2,1,0:T(8,128)S(1)}, u32[]{:S(2)}, u32[]{:S(2)}) async-start(f32[32,32,128]{2,1,0:T(8,128)} %fusion.24), calls=%async_computation.1 | async-start | bytes 1048576 | tf_op jit(solution)/shard_map/all_to_all | solution.py:127
  36.6 10.8 %copy-start.7 = (s32[256]{0:T(256)S(1)}, s32[256]{0:T(256)}, u32[]{:S(2)}) copy-start(s32[256]{0:T(256)} %param.8) | copy-start | bytes 3076
  44.1 6.0 %collective-permute-start = (f32[256,128]{0,1:T(8,128)S(1)}, f32[256,128]{0,1:T(8,128)S(1)}, u32[]{:S(2)}, u32[]{:S(2)}) collective-permute-start(f32[256,128]{0,1:T(8,128)S(1)} %fusion.53), channel_id=1, source_target_pairs={{0,1},{1,2},{2,3},{4,5},{5,6},{6,7},{8,9},{9,10},{10,11},{12,13},{... | collective-permute-start | bytes 393224 | tf_op jit(solution)/shard_map/ppermute | solution.py:21
  47.4 12.1 %copy-start.6 = (f32[256,128]{1,0:T(8,128)S(1)}, f32[256,128]{1,0:T(8,128)}, u32[]{:S(2)}) copy-start(f32[256,128]{1,0:T(8,128)} %param.10) | copy-start | bytes 393220
  86.8 15.9 %collective-permute-start.1 = (f32[256,128]{1,0:T(8,128)S(1)}, f32[256,128]{1,0:T(8,128)S(1)}, u32[]{:S(2)}, u32[]{:S(2)}) collective-permute-start(f32[256,128]{1,0:T(8,128)S(1)} %broadcast_divide_fusion.6), channel_id=1, source_target_pairs={{1,0},{2,1},{3,2},{5,4},{6,5},{7,6},{9,8},{10,9},{11,10},{13,12},{... | collective-permute-start | bytes 393224 | tf_op jit(solution)/shard_map/ppermute | solution.py:21
  108.4 21.4 %copy-start.5 = (s32[32,16,128]{2,1,0:T(8,128)S(1)}, s32[32,16,128]{2,1,0:T(8,128)}, u32[]{:S(2)}) copy-start(s32[32,16,128]{2,1,0:T(8,128)} %param.6) | copy-start | bytes 786436
  109.9 18.9 %all-to-all-start.2 = ((f32[32,32,128]{2,1,0:T(8,128)}), f32[32,32,128]{2,1,0:T(8,128)S(1)}, u32[]{:S(2)}, u32[]{:S(2)}) async-start(f32[32,32,128]{2,1,0:T(8,128)} %fusion.56), calls=%async_computation.2 | async-start | bytes 1048576 | tf_op jit(solution)/shard_map/all_to_all | solution.py:132
  156.0 28.2 %copy-start.1 = (f32[32,256,128]{1,2,0:T(8,128)S(1)}, f32[32,256,128]{1,2,0:T(8,128)}, u32[]{:S(2)}) copy-start(f32[32,256,128]{1,2,0:T(8,128)} %copy.25) | copy-start | bytes 12582916
  180.2 4.0 collective-permute-start.2
  216.9 5.7 %collective-permute-start.3 = (f32[256,128]{1,0:T(8,128)S(1)}, f32[256,128]{1,0:T(8,128)S(1)}, u32[]{:S(2)}, u32[]{:S(2)}) collective-permute-start(f32[256,128]{1,0:T(8,128)S(1)} %broadcast_divide_fusion.5), channel_id=1, source_target_pairs={{1,0},{2,1},{3,2},{5,4},{6,5},{7,6},{9,8},{10,9},{11,10},{13,12},{... | collective-permute-start | bytes 393224 | tf_op jit(solution)/shard_map/ppermute | solution.py:21
  275.0 31.0 %copy-start.2 = (f32[32,256,128]{1,2,0:T(8,128)S(1)}, f32[32,256,128]{1,2,0:T(8,128)}, u32[]{:S(2)}) copy-start(f32[32,256,128]{1,2,0:T(8,128)} %copy.25) | copy-start | bytes 12582916
  301.0 5.0 %collective-permute-start.4 = (f32[256,128]{0,1:T(8,128)S(1)}, f32[256,128]{0,1:T(8,128)S(1)}, u32[]{:S(2)}, u32[]{:S(2)}) collective-permute-start(f32[256,128]{0,1:T(8,128)S(1)} %fusion.51), channel_id=1, source_target_pairs={{0,1},{1,2},{2,3},{4,5},{5,6},{6,7},{8,9},{9,10},{10,11},{12,13},{... | collective-permute-start | bytes 393224 | tf_op jit(solution)/shard_map/ppermute | solution.py:21
  338.7 5.7 %collective-permute-start.5 = (f32[256,128]{1,0:T(8,128)S(1)}, f32[256,128]{1,0:T(8,128)S(1)}, u32[]{:S(2)}, u32[]{:S(2)}) collective-permute-start(f32[256,128]{1,0:T(8,128)S(1)} %broadcast_divide_fusion.4), channel_id=1, source_target_pairs={{1,0},{2,1},{3,2},{5,4},{6,5},{7,6},{9,8},{10,9},{11,10},{13,12},{... | collective-permute-start | bytes 393224 | tf_op jit(solution)/shard_map/ppermute | solution.py:21
  350.1 22.0 %copy-start.4 = (f32[32,128,128]{1,2,0:T(8,128)S(1)}, f32[32,128,128]{1,2,0:T(8,128)}, u32[]{:S(2)}) copy-start(f32[32,128,128]{1,2,0:T(8,128)} %get-tuple-element.14) | copy-start | bytes 6291460
  422.6 5.0 %collective-permute-start.6 = (f32[256,128]{0,1:T(8,128)S(1)}, f32[256,128]{0,1:T(8,128)S(1)}, u32[]{:S(2)}, u32[]{:S(2)}) collective-permute-start(f32[256,128]{0,1:T(8,128)S(1)} %fusion.50), channel_id=1, source_target_pairs={{0,1},{1,2},{2,3},{4,5},{5,6},{6,7},{8,9},{9,10},{10,11},{12,13},{... | collective-permute-start | bytes 393224 | tf_op jit(solution)/shard_map/ppermute | solution.py:21
  462.3 3.2 copy-start.3
